TPU v7x, 512 devices: a whole 4x4x16 slice. The times are simulated.
512 devices in a mesh: term: 16 (over z), doc: 32 (over x, y, core).
Axes of the slice: x: 4, y: 4, z: 16, core: 2. Of those that a mesh axis runs over, the one named last changes fastest.
Arguments:
- postings: bfloat16 [16384, 30720], P('doc', 'term'), may hold values from 0 to 3
- query_terms: int32 [128, 32], replicated, may hold values from 0 to 30719
- query_levels: int32 [128, 32], replicated, may hold values from 1 to 255
- feedback_ids: int32 [128, 10], replicated, may hold values from 0 to 16383, as said below
Outputs:
- first_scores: float32 [128, 16384], P('term', 'doc')
- final_scores: float32 [128, 16384], P('term', 'doc')
Inputs may be any that keep to these rules, and one draw needn't show every extreme that they name: `feedback_ids`: the 1280 feedback ids are all different.
All inputs are finite; a program needn't handle non-finite values.
Results may differ from a plain program's by a relative error of at most 0.0015.
Values may be sent and summed in bfloat16 or wider, within the bound.
No kernel may reach another device: no remote copies, remote signals or barrier semaphores. Data moves between devices by JAX's collectives and lax.ppermute only.
A program may use at most 64 MiB of HBM per device.

v0:
```python
import jax
import jax.numpy as jnp
from jax import lax
from jax.sharding import PartitionSpec as P

expansion_weight = 0.25


def query_slice(query_terms, query_levels, width, offset):
    columns = offset + lax.iota(jnp.int32, width)

    def add_term(position, total):
        ids_now = lax.dynamic_index_in_dim(query_terms, position, 1, keepdims=True)
        weight_now = (
            lax.dynamic_index_in_dim(query_levels, position, 1, keepdims=True).astype(jnp.float32)
            / 100.0
        )
        return total + jnp.where(ids_now == columns[None, :], weight_now, 0.0)

    initial = jnp.zeros((query_terms.shape[0], width), jnp.float32)
    return lax.fori_loop(0, query_terms.shape[1], add_term, initial)


def score_block(query_rows, postings):
    return lax.dot_general(
        query_rows, postings, (((1,), (1,)), ((), ())), preferred_element_type=jnp.float32
    )


def per_device(postings, query_terms, query_levels, feedback_ids):
    doc_rows, width = postings.shape
    queries = query_terms.shape[0]
    term_groups = lax.axis_size("term")
    group_rows = queries // term_groups
    term_index = lax.axis_index("term")
    doc_index = lax.axis_index("doc")
    query_part = query_slice(query_terms, query_levels, width, term_index * width)
    query_rounded = query_part.astype(jnp.bfloat16)
    local_slot = feedback_ids - doc_index * doc_rows
    positions = lax.iota(jnp.int32, doc_rows)
    selector = (local_slot[:, :, None] == positions[None, None, :]).astype(jnp.float32)
    partial_scores = score_block(query_rounded, postings)
    first_all = lax.psum(partial_scores, "term")
    first_scores = lax.dynamic_slice_in_dim(first_all, term_index * group_rows, group_rows, 0)
    feedback = jnp.sum(selector * first_all[:, None, :], axis=2).astype(jnp.bfloat16)
    feedback_wide = feedback.astype(jnp.float32)
    mixing = jnp.sum(selector * feedback_wide[:, :, None], axis=1).astype(jnp.bfloat16)
    numerator = jnp.dot(mixing, postings, preferred_element_type=jnp.float32)
    weight_part = jnp.sum(feedback_wide, axis=1)
    numerator_all, weight_sum = lax.psum((numerator, weight_part), "doc")
    expanded = (query_part + expansion_weight * numerator_all / weight_sum[:, None]).astype(
        jnp.bfloat16
    )
    final_scores = lax.psum_scatter(
        score_block(expanded, postings), "term", scatter_dimension=0, tiled=True
    )
    return (first_scores, final_scores)


def solution(mesh):
    return jax.shard_map(
        per_device,
        mesh=mesh,
        in_specs=(P("doc", "term"), P(), P(), P()),
        out_specs=(P("term", "doc"), P("term", "doc")),
        check_vma=False,
    )
```

profile of v0, /device:TPU:6, one launch (start us, length us, event | category | flops | bytes accessed | tf_op | source)
XLA Modules:
  0.0 416.9 jit_solution(17886859265091422871)
XLA Ops:
  7.2 53.6 %while.14 = (s32[]{:T(128)}, f32[128,1920]{1,0:T(8,128)S(1)}, s32[128,32]{0,1:T(8,128)}, s32[128,32]{0,1:T(8,128)}, s32[]{:T(128)}, /*index=5*/s32[]{:T(128)}, s32[]{:T(128)}) while((s32[]{:T(128)}, f32[128,1920]{1,0:T(8,128)S(1)}, s32[128,32]{0,1:T(8,128)}, s32[128,32]{0,1:T(8,128)}, s32[]{:T(128)}, /*index=5*/s32[]{:T(128)}, ...), condition=%wide.region_1.2_spmd.clone, body=%wide.region_0.1_spmd.clone.sunk | while | flops 985219 | bytes 1984619 | solution.py:21
  7.3 0.8 multiply_bitcast_fusion.2
  9.1 0.7 multiply_bitcast_fusion.2
  10.7 0.7 multiply_bitcast_fusion.2
  14.1 0.7 multiply_bitcast_fusion.2
  15.7 0.7 multiply_bitcast_fusion.2
  17.4 0.7 multiply_bitcast_fusion.2
  19.1 0.7 multiply_bitcast_fusion.2
  22.4 0.7 multiply_bitcast_fusion.2
  24.1 0.7 multiply_bitcast_fusion.2
  27.4 0.7 multiply_bitcast_fusion.2
  29.1 0.7 multiply_bitcast_fusion.2
  32.4 0.7 multiply_bitcast_fusion.2
  34.1 0.7 multiply_bitcast_fusion.2
  35.8 0.7 multiply_bitcast_fusion.2
  37.5 0.7 multiply_bitcast_fusion.2
  40.8 0.7 multiply_bitcast_fusion.2
  42.5 0.7 multiply_bitcast_fusion.2
  45.8 0.7 multiply_bitcast_fusion.2
  47.5 0.7 multiply_bitcast_fusion.2
  49.2 0.7 multiply_bitcast_fusion.2
  50.8 0.7 multiply_bitcast_fusion.2
  54.2 0.7 multiply_bitcast_fusion.2
  60.9 1.5 fusion.5
  62.4 140.0 %all-reduce.3.cloned.1.call-done = f32[128,512]{1,0:T(8,128)} async-done(((f32[128,512]{1,0:T(8,128)}), f32[128,512]{1,0:T(8,128)}) %all-reduce.3.cloned.1.call-update) | async-done | bytes 262160 | tf_op jit(solution)/shard_map/psum | solution.py:43
  202.4 1.5 select_reduce_fusion.1
  204.4 1.4 fusion.11
  205.9 53.0 %psum.23 = f32[128]{0:T(128)S(1)} all-reduce(f32[128]{0:T(128)S(1)} %fusion.9), channel_id=1, replica_groups=mesh['term'=16,'doc'=32] {'doc'}, use_global_device_ids=true, to_apply=%region_7.8 | all-reduce | flops 128 | bytes 1024 | tf_op jit(solution)/shard_map/psum | solution.py:50
  258.9 79.8 %all-reduce.5.cloned.1.call-done = f32[128,1920]{1,0:T(8,128)} async-done(((f32[128,1920]{1,0:T(8,128)}), f32[128,1920]{1,0:T(8,128)}) %all-reduce.5.cloned.1.call-update) | async-done | bytes 983056 | tf_op jit(solution)/shard_map/psum | solution.py:50
  338.7 2.7 fusion.2
  341.4 1.3 constant_dynamic-slice_fusion
  342.8 67.6 %reduce-scatter.2.cloned.1.call-done = f32[8,512]{1,0:T(8,128)} async-done(((f32[128,512]{1,0:T(8,128)}), f32[8,512]{1,0:T(8,128)}) %reduce-scatter.2.cloned.1.call-update) | async-done | bytes 16400 | tf_op jit(solution)/shard_map/reduce_scatter | solution.py:54
  (121 shorter events, 37.9 us)
Async XLA Ops:
  7.2 53.7 %copy-start = (bf16[512,1920]{1,0:T(8,128)(2,1)S(1)}, bf16[512,1920]{1,0:T(8,128)(2,1)}, u32[]{:S(2)}) copy-start(bf16[512,1920]{1,0:T(8,128)(2,1)} %param.6) | copy-start | bytes 5898244
  7.2 195.3 %all-reduce.3.cloned.1.call-start = ((), (), s32[]{:S(2)}) async-start(), calls=%async_computation.1 | async-start | bytes 524288 | tf_op jit(solution)/shard_map/psum | solution.py:43
  60.8 1.6 copy-start.1
  62.4 276.4 %all-reduce.5.cloned.1.call-start = ((), (), s32[]{:S(2)}) async-start(), calls=%async_computation.2 | async-start | bytes 1966080 | tf_op jit(solution)/shard_map/psum | solution.py:50
  205.8 204.5 %reduce-scatter.2.cloned.1.call-start = ((), (), s32[]{:S(2)}) async-start(), calls=%async_computation.3 | async-start | bytes 278528 | tf_op jit(solution)/shard_map/reduce_scatter | solution.py:54
Sparse Core Ops, SparseCore 0:
  62.5 139.9 all-reduce.2
  206.0 132.6 all-reduce.4
  342.1 68.2 reduce-scatter.1
where the time goes:
time: 420 us; the launch traced here: 417 us
  waiting for transfers between devices  287 us (68%)
  blocking collectives  53 us (13%)
  other arithmetic  32.6 us (8%)
  local copies, waits for them, and re-layouts  23.5 us (6%)
  between operations  13.8 us (3%)
  matrix products  5.59 us (1%)
    psum x1, waiting for transfers between devices, per_device(): first_all = lax.psum(partial_scores, 'term')  140 us
    psum x1, waiting for transfers between devices, per_device(): numerator_all, weight_sum = lax.psum((numerator, weight_part), 'doc')  79.8 us
    reduce_scatter x1, waiting for transfers between devices, per_device(): lax.psum_scatter(score_block(expanded, postings), 'term', scatter_dimensi...  67.6 us
    psum x1, blocking collectives, per_device(): numerator_all, weight_sum = lax.psum((numerator, weight_part), 'doc')  53 us
    broadcast_in_dim x32, other arithmetic, add_term(): return total + jnp.where(ids_now == columns[None, :], weight_now, 0.0)  22.5 us
    eq x32, local copies, waits for them, and re-layouts, add_term(): return total + jnp.where(ids_now == columns[None, :], weight_now, 0.0)  22.1 us
  transfers between devices with their start and end apart: 3, of which 3 were waited for; matrix products, arithmetic and copies ran while one was open for 0% of the time, Pallas kernels for 0%

commit v1 on v0

--- a/solution.py
+++ b/solution.py
@@ -28,6 +28,19 @@
 
 
 def per_device(postings, query_terms, query_levels, feedback_ids):
+
+    def return_all_sources_all_all(point):
+        axis_n = jax.lax.axis_size("term")
+        small, w_next = (point, 0)
+        while 1 << w_next < axis_n:
+            steps_seen = []
+            for t in [*range(axis_n)]:
+                steps_seen.append((t, t ^ 1 << w_next))
+            met_up = jax.lax.ppermute(small, axis_name="term", perm=steps_seen)
+            small = small + met_up
+            w_next = w_next + 1
+        return small
+
     doc_rows, width = postings.shape
     queries = query_terms.shape[0]
     term_groups = lax.axis_size("term")
@@ -40,7 +53,7 @@
     positions = lax.iota(jnp.int32, doc_rows)
     selector = (local_slot[:, :, None] == positions[None, None, :]).astype(jnp.float32)
     partial_scores = score_block(query_rounded, postings)
-    first_all = lax.psum(partial_scores, "term")
+    first_all = return_all_sources_all_all(partial_scores)
     first_scores = lax.dynamic_slice_in_dim(first_all, term_index * group_rows, group_rows, 0)
     feedback = jnp.sum(selector * first_all[:, None, :], axis=2).astype(jnp.bfloat16)
     feedback_wide = feedback.astype(jnp.float32)

time: 420 us -> 371 us (0.88)
  waiting for transfers between devices: 287 us -> 200 us
  starting transfers between devices: 0.12 us -> 37.1 us
    psum x1 -> x0, waiting for transfers between devices: 140 us -> none  [per_device(): first_all = lax.psum(partial_scores, 'term')]
    ppermute x0 -> x4, waiting for transfers between devices: none -> 53.6 us  [return_all_sources_all_all(): met_up = jax.lax.ppermute(small, axis_name='term', perm=steps_seen)]
    ppermute x0 -> x4, starting transfers between devices: none -> 37 us  [return_all_sources_all_all(): met_up = jax.lax.ppermute(small, axis_name='term', perm=steps_seen)]
  transfers between devices with their start and end apart: 3 -> 6, of which waited for: 3 -> 6; matrix products, arithmetic and copies ran while one was open for 0% -> 0% of each run, Pallas kernels for 0% -> 0%
where the time goes in v1:
time: 371 us; the launch traced here: 368 us
  waiting for transfers between devices  200 us (54%)
  blocking collectives  56 us (15%)
  starting transfers between devices  37.1 us (10%)
  other arithmetic  32.8 us (9%)
  local copies, waits for them, and re-layouts  22.7 us (6%)
  between operations  14.2 us (4%)
  matrix products  4.9 us (1%)
    psum x1, waiting for transfers between devices, per_device(): numerator_all, weight_sum = lax.psum((numerator, weight_part), 'doc')  77.8 us
    reduce_scatter x1, waiting for transfers between devices, per_device(): lax.psum_scatter(score_block(expanded, postings), 'term', scatter_dimensi...  68.5 us
    psum x1, blocking collectives, per_device(): numerator_all, weight_sum = lax.psum((numerator, weight_part), 'doc')  56 us
    ppermute x4, waiting for transfers between devices, return_all_sources_all_all(): met_up = jax.lax.ppermute(small, axis_name='term', perm=steps_seen)  53.6 us
    ppermute x4, starting transfers between devices, return_all_sources_all_all(): met_up = jax.lax.ppermute(small, axis_name='term', perm=steps_seen)  37 us
    broadcast_in_dim x32, other arithmetic, add_term(): return total + jnp.where(ids_now == columns[None, :], weight_now, 0.0)  22.5 us
    eq x32, local copies, waits for them, and re-layouts, add_term(): return total + jnp.where(ids_now == columns[None, :], weight_now, 0.0)  22.1 us
    add x32, other arithmetic, add_term(): return total + jnp.where(ids_now == columns[None, :], weight_now, 0.0)  8.05 us
  transfers between devices with their start and end apart: 6, of which 6 were waited for; matrix products, arithmetic and copies ran while one was open for 0% of the time, Pallas kernels for 0%

profile of v1, /device:TPU:6, one launch (start us, length us, event | category | flops | bytes accessed | tf_op | source)
XLA Modules:
  0.0 368.4 jit_solution(8282652637267309129)
XLA Ops:
  7.2 53.6 %while.14 = (s32[]{:T(128)}, f32[128,1920]{1,0:T(8,128)S(1)}, s32[128,32]{0,1:T(8,128)}, s32[128,32]{0,1:T(8,128)}, s32[]{:T(128)}, /*index=5*/s32[]{:T(128)}, s32[]{:T(128)}) while((s32[]{:T(128)}, f32[128,1920]{1,0:T(8,128)S(1)}, s32[128,32]{0,1:T(8,128)}, s32[128,32]{0,1:T(8,128)}, s32[]{:T(128)}, /*index=5*/s32[]{:T(128)}, ...), condition=%wide.region_1.2_spmd.clone, body=%wide.region_0.1_spmd.clone.sunk | while | flops 985219 | bytes 1984619 | solution.py:21
  7.3 0.8 multiply_bitcast_fusion.2
  9.1 0.7 multiply_bitcast_fusion.2
  10.7 0.7 multiply_bitcast_fusion.2
  14.1 0.7 multiply_bitcast_fusion.2
  15.7 0.7 multiply_bitcast_fusion.2
  17.4 0.7 multiply_bitcast_fusion.2
  19.1 0.7 multiply_bitcast_fusion.2
  22.4 0.7 multiply_bitcast_fusion.2
  24.1 0.7 multiply_bitcast_fusion.2
  27.4 0.7 multiply_bitcast_fusion.2
  29.1 0.7 multiply_bitcast_fusion.2
  32.4 0.7 multiply_bitcast_fusion.2
  34.1 0.7 multiply_bitcast_fusion.2
  35.8 0.7 multiply_bitcast_fusion.2
  37.5 0.7 multiply_bitcast_fusion.2
  40.8 0.7 multiply_bitcast_fusion.2
  60.9 0.8 fusion.5
  61.6 3.8 %collective-permute-start = (f32[128,512]{1,0:T(8,128)S(1)}, f32[128,512]{1,0:T(8,128)S(1)}, u32[]{:S(2)}, u32[]{:S(2)}) collective-permute-start(f32[128,512]{1,0:T(8,128)S(1)} %fusion.5), channel_id=1, source_target_pairs={{0,32},{32,0},{64,96},{96,64},{128,160},{160,128},{192,224},{224,1... | collective-permute-start | bytes 786440 | tf_op jit(solution)/shard_map/ppermute | solution.py:39
  65.5 6.3 %collective-permute-done = f32[128,512]{1,0:T(8,128)S(1)} collective-permute-done((f32[128,512]{1,0:T(8,128)S(1)}, f32[128,512]{1,0:T(8,128)S(1)}, u32[]{:S(2)}, u32[]{:S(2)}) %collective-permute-start) | collective-permute-done | bytes 262176 | tf_op jit(solution)/shard_map/ppermute | solution.py:39
  71.8 5.2 %collective-permute-start.1 = (f32[128,512]{1,0:T(8,128)S(1)}, f32[128,512]{1,0:T(8,128)S(1)}, u32[]{:S(2)}, u32[]{:S(2)}) collective-permute-start(f32[128,512]{1,0:T(8,128)S(1)} %add.62), channel_id=1, source_target_pairs={{0,64},{32,96},{64,0},{96,32},{128,192},{160,224},{192,128},{224,1... | collective-permute-start | bytes 786440 | tf_op jit(solution)/shard_map/ppermute | solution.py:39
  77.0 11.2 %collective-permute-done.1 = f32[128,512]{1,0:T(8,128)S(1)} collective-permute-done((f32[128,512]{1,0:T(8,128)S(1)}, f32[128,512]{1,0:T(8,128)S(1)}, u32[]{:S(2)}, u32[]{:S(2)}) %collective-permute-start.1) | collective-permute-done | bytes 262176 | tf_op jit(solution)/shard_map/ppermute | solution.py:39
  88.3 9.1 %collective-permute-start.2 = (f32[128,512]{1,0:T(8,128)S(1)}, f32[128,512]{1,0:T(8,128)S(1)}, u32[]{:S(2)}, u32[]{:S(2)}) collective-permute-start(f32[128,512]{1,0:T(8,128)S(1)} %add.63), channel_id=1, source_target_pairs={{0,128},{32,160},{64,192},{96,224},{128,0},{160,32},{192,64},{224,... | collective-permute-start | bytes 786440 | tf_op jit(solution)/shard_map/ppermute | solution.py:39
  97.4 21.3 %collective-permute-done.2 = f32[128,512]{1,0:T(8,128)S(1)} collective-permute-done((f32[128,512]{1,0:T(8,128)S(1)}, f32[128,512]{1,0:T(8,128)S(1)}, u32[]{:S(2)}, u32[]{:S(2)}) %collective-permute-start.2) | collective-permute-done | bytes 262176 | tf_op jit(solution)/shard_map/ppermute | solution.py:39
  118.7 18.9 %collective-permute-start.3 = (f32[128,512]{1,0:T(8,128)S(1)}, f32[128,512]{1,0:T(8,128)}, u32[]{:S(2)}, u32[]{:S(2)}) collective-permute-start(f32[128,512]{1,0:T(8,128)S(1)} %add.64), channel_id=1, source_target_pairs={{0,256},{32,288},{64,320},{96,352},{128,384},{160,416},{192,448},{... | collective-permute-start | bytes 786440 | tf_op jit(solution)/shard_map/ppermute | solution.py:39
  137.7 14.8 %collective-permute-done.3 = f32[128,512]{1,0:T(8,128)} collective-permute-done((f32[128,512]{1,0:T(8,128)S(1)}, f32[128,512]{1,0:T(8,128)}, u32[]{:S(2)}, u32[]{:S(2)}) %collective-permute-start.3) | collective-permute-done | bytes 262176 | tf_op jit(solution)/shard_map/ppermute | solution.py:39
  152.4 1.0 add.65
  154.4 1.4 fusion.11
  156.0 56.0 %psum.15 = f32[128]{0:T(128)S(1)} all-reduce(f32[128]{0:T(128)S(1)} %fusion.9), channel_id=1, replica_groups=mesh['term'=16,'doc'=32] {'doc'}, use_global_device_ids=true, to_apply=%region_6.7 | all-reduce | flops 128 | bytes 1024 | tf_op jit(solution)/shard_map/psum | solution.py:63
  212.0 77.8 %all-reduce.2.cloned.1.call-done = f32[128,1920]{1,0:T(8,128)} async-done(((f32[128,1920]{1,0:T(8,128)}), f32[128,1920]{1,0:T(8,128)}) %all-reduce.2.cloned.1.call-update) | async-done | bytes 983056 | tf_op jit(solution)/shard_map/psum | solution.py:63
  289.7 2.7 fusion.2
  293.1 68.5 %reduce-scatter.2.cloned.1.call-done = f32[8,512]{1,0:T(8,128)} async-done(((f32[128,512]{1,0:T(8,128)}), f32[8,512]{1,0:T(8,128)}) %reduce-scatter.2.cloned.1.call-update) | async-done | bytes 16400 | tf_op jit(solution)/shard_map/reduce_scatter | solution.py:67
  (130 shorter events, 43.3 us)
Async XLA Ops:
  7.2 53.7 %copy-start = (bf16[512,1920]{1,0:T(8,128)(2,1)S(1)}, bf16[512,1920]{1,0:T(8,128)(2,1)}, u32[]{:S(2)}) copy-start(bf16[512,1920]{1,0:T(8,128)(2,1)} %param.6) | copy-start | bytes 5898244
  7.2 282.5 %all-reduce.2.cloned.1.call-start = ((), (), s32[]{:S(2)}) async-start(), calls=%async_computation.1 | async-start | bytes 1966080 | tf_op jit(solution)/shard_map/psum | solution.py:63
  61.6 76.0 %copy-start.1 = (s32[128,10]{0,1:T(8,128)S(1)}, s32[128,10]{0,1:T(8,128)}, u32[]{:S(2)}) copy-start(s32[128,10]{0,1:T(8,128)} %param.9) | copy-start | bytes 15364
  61.6 10.1 %collective-permute-start = (f32[128,512]{1,0:T(8,128)S(1)}, f32[128,512]{1,0:T(8,128)S(1)}, u32[]{:S(2)}, u32[]{:S(2)}) collective-permute-start(f32[128,512]{1,0:T(8,128)S(1)} %fusion.5), channel_id=1, source_target_pairs={{0,32},{32,0},{64,96},{96,64},{128,160},{160,128},{192,224},{224,1... | collective-permute-start | bytes 786440 | tf_op jit(solution)/shard_map/ppermute | solution.py:39
  71.8 16.4 %collective-permute-start.1 = (f32[128,512]{1,0:T(8,128)S(1)}, f32[128,512]{1,0:T(8,128)S(1)}, u32[]{:S(2)}, u32[]{:S(2)}) collective-permute-start(f32[128,512]{1,0:T(8,128)S(1)} %add.62), channel_id=1, source_target_pairs={{0,64},{32,96},{64,0},{96,32},{128,192},{160,224},{192,128},{224,1... | collective-permute-start | bytes 786440 | tf_op jit(solution)/shard_map/ppermute | solution.py:39
  88.3 30.4 %collective-permute-start.2 = (f32[128,512]{1,0:T(8,128)S(1)}, f32[128,512]{1,0:T(8,128)S(1)}, u32[]{:S(2)}, u32[]{:S(2)}) collective-permute-start(f32[128,512]{1,0:T(8,128)S(1)} %add.63), channel_id=1, source_target_pairs={{0,128},{32,160},{64,192},{96,224},{128,0},{160,32},{192,64},{224,... | collective-permute-start | bytes 786440 | tf_op jit(solution)/shard_map/ppermute | solution.py:39
  118.7 33.7 %collective-permute-start.3 = (f32[128,512]{1,0:T(8,128)S(1)}, f32[128,512]{1,0:T(8,128)}, u32[]{:S(2)}, u32[]{:S(2)}) collective-permute-start(f32[128,512]{1,0:T(8,128)S(1)} %add.64), channel_id=1, source_target_pairs={{0,256},{32,288},{64,320},{96,352},{128,384},{160,416},{192,448},{... | collective-permute-start | bytes 786440 | tf_op jit(solution)/shard_map/ppermute | solution.py:39
  155.9 205.7 %reduce-scatter.2.cloned.1.call-start = ((), (), s32[]{:S(2)}) async-start(), calls=%async_computation.2 | async-start | bytes 278528 | tf_op jit(solution)/shard_map/reduce_scatter | solution.py:67
Sparse Core Ops, SparseCore 0:
  156.0 133.6 all-reduce.1
  293.3 68.2 reduce-scatter.1
